TPU v7x, 32 devices: a whole 2x2x4 slice. The times are simulated.
32 devices in a mesh: ab: 4 (over y, x), cd: 4 (over z), ij: 2 (over core).
Axes of the slice: x: 2, y: 2, z: 4, core: 2. Of those that a mesh axis runs over, the one named last changes fastest.
Arguments:
- amplitudes: float32 [512, 4096], P('ij', ('cd', 'ab')), may hold values from -6 to 6
- integrals: float32 [256, 256, 256], P(('ab', 'cd')), may hold values from -0.375 to 0.375
- tile_row: int32 [256], P(('ab', 'cd')), may hold values from 0 to 3, as said below
- tile_col: int32 [256], P(('ab', 'cd')), may hold values from 0 to 3
- tile_count: int32 [16], P(('ab', 'cd')), may hold values from 1 to 16, as said below
Outputs:
- residual: float32 [512, 4, 16, 64], P('ij', 'ab', 'cd')
Inputs may be any that keep to these rules, and one draw needn't show every extreme that they name: Within one slab the 16 slots name distinct (tile_row, tile_col) pairs. `tile_count`: in every draw some slab has all 16 slots live.
All inputs are finite; a program needn't handle non-finite values.
Results may differ from a plain program's by a relative error of at most 0.0003.
Values sent between devices are 32-bit elements; how exact they have to be, the bound alone decides.
A program may use at most 128 MiB of HBM per device.

v0:
```python
import functools
import math

import jax
import jax.numpy as jnp
from jax import lax
from jax.experimental import pallas as pl
from jax.experimental.pallas import tpu as pltpu
from jax.sharding import PartitionSpec as P

MESH = pl.DeviceIdType.MESH
LANES = 128
VMEM_BYTES = 63 * 1024 * 1024


def split(value):
    high = value.astype(jnp.bfloat16)
    low = (value - high.astype(jnp.float32)).astype(jnp.bfloat16)
    return high, low


def ladder_kernel(
    n_ab, n_cd, block, chunks,
    row_ref, col_ref, count_ref, amp_ref, tiles_ref, out_ref,
    tiles, w_high, w_low, gathered, a_both, partial, up_in, down_in, up_out, down_out,
    summed, outgoing, mirrored,
    tile_sem, own_sem, ag_send, ag_recv, up_send, up_recv, down_send, down_recv,
    mi_send, mi_recv,
):
    me_ab, me_cd, me_ij = lax.axis_index("ab"), lax.axis_index("cd"), lax.axis_index("ij")
    slots, size = tiles_ref.shape[0], tiles_ref.shape[1]
    group = block // n_cd
    rows = group * n_ab * block
    targets = n_ab * n_cd
    piece = group * group
    own_place = me_ab * n_cd + me_cd

    tile_copies = [
        pltpu.make_async_copy(tiles_ref.at[k], tiles.at[k], tile_sem.at[k]) for k in range(slots)
    ]
    for copy in tile_copies:
        copy.start()
    own = pltpu.make_async_copy(amp_ref, gathered.at[0], own_sem)
    own.start()

    barrier = pltpu.get_barrier_semaphore()
    for j in range(1, n_ab):
        pl.semaphore_signal(
            barrier, inc=1, device_id=(lax.rem(me_ab + j, n_ab), me_cd, me_ij), device_id_type=MESH
        )
    pl.semaphore_signal(barrier, inc=1, device_id=(me_ab, me_cd, 1 - me_ij), device_id_type=MESH)

    @pl.when(me_cd > 0)
    def _():
        pl.semaphore_signal(barrier, inc=1, device_id=(me_ab, me_cd - 1, me_ij), device_id_type=MESH)

    @pl.when(me_cd < n_cd - 1)
    def _():
        pl.semaphore_signal(barrier, inc=1, device_id=(me_ab, me_cd + 1, me_ij), device_id_type=MESH)

    ends = jnp.where(me_cd > 0, 1, 0) + jnp.where(me_cd < n_cd - 1, 1, 0)
    pl.semaphore_wait(barrier, n_ab + ends)

    ag = {}
    for h in range(chunks):
        part = pl.ds(h * LANES, LANES)
        for j in range(1, n_ab):
            ag[h, j] = pltpu.make_async_remote_copy(
                src_ref=amp_ref.at[part],
                dst_ref=gathered.at[j, part],
                send_sem=ag_send.at[h, j],
                recv_sem=ag_recv.at[h, j],
                device_id=(lax.rem(me_ab + j, n_ab), me_cd, me_ij),
                device_id_type=MESH,
            )
            if h == 0:
                ag[h, j].start()

    keys = [row_ref[k] * n_ab + col_ref[k] for k in range(slots)]
    live_count = count_ref[0]
    for copy in tile_copies:
        copy.wait()
    for j in range(n_ab):
        column = lax.rem(me_ab - j + n_ab, n_ab)
        for r in range(n_ab):
            slot = jnp.int32(0)
            for k in range(1, slots):
                slot = jnp.where(keys[k] == r * n_ab + column, jnp.int32(k), slot)
            scale = jnp.where(slot < live_count, jnp.float32(1), jnp.float32(0))
            high, low = split(tiles[slot] * scale)
            at = (slice(None), pl.ds(r * block, block), pl.ds(j * size, size))
            w_high[at] = high.reshape(block, block, size)
            w_low[at] = low.reshape(block, block, size)

    own.wait()
    mi = {}
    contract = (((1,), (1,)), ((), ()))
    last = n_cd - 1

    def up(h, d, source):
        return pltpu.make_async_remote_copy(
            src_ref=source.at[h, d],
            dst_ref=up_in.at[h, d],
            send_sem=up_send.at[h, d],
            recv_sem=up_recv.at[h, d],
            device_id=(me_ab, me_cd + 1, me_ij),
            device_id_type=MESH,
        )

    def down(h, d, source):
        return pltpu.make_async_remote_copy(
            src_ref=source.at[h, d],
            dst_ref=down_in.at[h, d],
            send_sem=down_send.at[h, d],
            recv_sem=down_recv.at[h, d],
            device_id=(me_ab, me_cd - 1, me_ij),
            device_id_type=MESH,
        )

    def compute(h):
        part = pl.ds(h * LANES, LANES)
        for j in range(n_ab):
            if j:
                ag[h, j].wait_recv()
                if h + 1 < chunks:
                    ag[h + 1, j].start()
            high, low = split(gathered[j, part])
            a_both[pl.ds(0, LANES), pl.ds(j * size, size)] = high
            a_both[pl.ds(LANES, LANES), pl.ds(j * size, size)] = low
        for i in range(n_cd):
            d = jnp.where(me_cd < n_cd // 2, last - i, i)
            lead = pl.ds(d * group, group)
            left_high = w_high[lead].reshape(rows, n_ab * size)
            left_low = w_low[lead].reshape(rows, n_ab * size)
            right = a_both[...]
            wide = lax.dot_general(left_high, right, contract, preferred_element_type=jnp.float32)
            value = wide[:, LANES:] + lax.dot_general(
                left_low, right[:LANES], contract, preferred_element_type=jnp.float32
            )
            value += wide[:, :LANES]
            partial[h, d] = value
            if i < last:

                @pl.when(me_cd == 0)
                def _():
                    up(h, d, partial).start()

                @pl.when(me_cd == last)
                def _():
                    down(h, d, partial).start()

    def relay(h, step):
        for_up = last + me_cd - step

        @pl.when((me_cd >= 1) & (me_cd <= step))
        def _():
            up(h, for_up, up_out).wait_recv()
            if step < last:
                up_out[h, for_up] = partial[h, for_up] + up_in[h, for_up]
                up(h, for_up, up_out).start()

        for_down = step - last + me_cd

        @pl.when((me_cd < last) & (for_down >= 0))
        def _():
            down(h, for_down, down_out).wait_recv()
            if step < last:
                down_out[h, for_down] = partial[h, for_down] + down_in[h, for_down]
                down(h, for_down, down_out).start()

    def finish(h):
        summed[h] = partial[h, me_cd]

        @pl.when(me_cd > 0)
        def _():
            summed[h] += up_in[h, me_cd]

        @pl.when(me_cd < last)
        def _():
            summed[h] += down_in[h, me_cd]

        for x in range(group):
            for y in range(group):
                outgoing[h, pl.ds(x * group + y, targets, stride=piece), :] = summed[
                    h, pl.ds(x * n_ab * block + y, targets, stride=group), :
                ]
        for i in range(n_cd):
            q = jnp.where(me_cd < n_cd // 2, last - i, i)
            for j in range(n_ab):
                p = lax.rem(me_ab + j, n_ab)
                t = p * n_cd + q
                mi[h, i, j] = pltpu.make_async_remote_copy(
                    src_ref=outgoing.at[h, pl.ds(t * piece, piece)],
                    dst_ref=mirrored.at[h, pl.ds(own_place * piece, piece)],
                    send_sem=mi_send.at[h, t],
                    recv_sem=mi_recv.at[h, own_place],
                    device_id=(p, q, 1 - me_ij),
                    device_id_type=MESH,
                )
                mi[h, i, j].start()

    waiting = None
    for h in range(chunks):
        compute(h)
        if waiting is not None:
            for step in range(2, n_cd):
                relay(waiting, step)
            finish(waiting)
        relay(h, 1)
        waiting = h
    for step in range(2, n_cd):
        relay(waiting, step)
    finish(waiting)
    for h in range(chunks):
        for s in range(targets):
            pltpu.make_async_remote_copy(
                src_ref=outgoing.at[h, pl.ds(s * piece, piece)],
                dst_ref=mirrored.at[h, pl.ds(s * piece, piece)],
                send_sem=mi_send.at[h, s],
                recv_sem=mi_recv.at[h, s],
                device_id=(me_ab, me_cd, 1 - me_ij),
                device_id_type=MESH,
            ).wait_recv()
        for y in range(group):
            out_ref[y, :, pl.ds(h * LANES, LANES)] = (
                summed[h, pl.ds(y * n_ab * block, n_ab * block), :]
                + mirrored[h, pl.ds(y, targets * group, stride=group), :]
            )
    for h in range(chunks):
        for d in range(n_cd):

            @pl.when(me_cd < d)
            def _():
                up(h, d, up_out).wait_send()

            @pl.when(me_cd > d)
            def _():
                down(h, d, down_out).wait_send()

    for copy in [*ag.values(), *mi.values()]:
        copy.wait_send()


def fused(amplitudes, integrals, tile_row, tile_col, tile_count):
    occ_dev = amplitudes.shape[0]
    slots, size = integrals.shape[0], integrals.shape[1]
    block = math.isqrt(size)
    n_ab, n_cd = lax.axis_size("ab"), lax.axis_size("cd")
    group = block // n_cd
    rows = group * n_ab * block
    chunks = occ_dev // LANES
    targets = n_ab * n_cd
    piece = group * group
    f32, bf16 = jnp.float32, jnp.bfloat16
    dma = pltpu.SemaphoreType.DMA
    out = pl.pallas_call(
        functools.partial(ladder_kernel, n_ab, n_cd, block, chunks),
        out_shape=jax.ShapeDtypeStruct((group, n_ab * block, occ_dev), f32),
        in_specs=[pl.BlockSpec(memory_space=pltpu.SMEM)] * 3
        + [pl.BlockSpec(memory_space=pl.ANY)] * 2,
        out_specs=pl.BlockSpec(memory_space=pltpu.VMEM),
        scratch_shapes=[
            pltpu.VMEM((slots, size, size), f32),
            pltpu.VMEM((block, n_ab * block, n_ab * size), bf16),
            pltpu.VMEM((block, n_ab * block, n_ab * size), bf16),
            pltpu.VMEM((n_ab, occ_dev, size), f32),
            pltpu.VMEM((2 * LANES, n_ab * size), bf16),
            *[pltpu.VMEM((chunks, n_cd, rows, LANES), f32)] * 5,
            pltpu.VMEM((chunks, rows, LANES), f32),
            pltpu.VMEM((chunks, targets * piece, LANES), f32),
            pltpu.VMEM((chunks, targets * piece, LANES), f32),
            dma((slots,)),
            dma,
            dma((chunks, n_ab)),
            dma((chunks, n_ab)),
            *[dma((chunks, n_cd))] * 4,
            dma((chunks, targets)),
            dma((chunks, targets)),
        ],
        compiler_params=pltpu.CompilerParams(
            collective_id=0, has_side_effects=True, vmem_limit_bytes=VMEM_BYTES
        ),
    )(tile_row, tile_col, tile_count, amplitudes, integrals)
    return jnp.transpose(out, (2, 0, 1))[:, None]


def from_partner(block, axis, bit):
    count = lax.axis_size(axis)
    route = []
    for low in range(count):
        high = low | 1 << bit
        if high != low and high < count:
            route += [(low, high), (high, low)]
    return lax.ppermute(block, axis, route)


def place_rows(chosen, tile_rows, row_picks, block_size):
    terms = jnp.einsum("okf,kef->oke", chosen, tile_rows, precision=lax.Precision.HIGHEST)
    occ_dev, slots, width = terms.shape
    terms = terms.reshape(occ_dev, slots, width // block_size, block_size)
    placed = jnp.einsum("rk,okab->aorb", row_picks, terms, precision=lax.Precision.HIGHEST)
    return placed.reshape(width // block_size, occ_dev, row_picks.shape[0] * block_size)


def general(amplitudes, integrals, tile_row, tile_col, tile_count):
    occ_dev = amplitudes.shape[0]
    slots = integrals.shape[0]
    tile_size = integrals.shape[1]
    block_size = math.isqrt(tile_size)
    blocks = lax.axis_size("ab")
    cd_size = lax.axis_size("cd")
    group_size = block_size // cd_size
    live_count = tile_count[0]
    live = jnp.arange(slots, dtype=jnp.int32) < live_count
    row_picks = (
        (tile_row[None, :] == jnp.arange(blocks, dtype=jnp.int32)[:, None]) & live[None, :]
    ).astype(jnp.float32)
    gathered = lax.all_gather(amplitudes, "ab", axis=1, tiled=True)
    columns = gathered.reshape(occ_dev, -1, tile_size)
    chosen = jnp.take(columns, tile_col, axis=1)
    partial_value = place_rows(chosen, integrals, row_picks, block_size)
    summed = lax.psum_scatter(partial_value, "cd", scatter_dimension=0, tiled=True)
    direct = jnp.transpose(summed, (1, 0, 2))
    outgoing = summed.reshape(group_size, occ_dev, blocks, cd_size, group_size)
    outgoing = jnp.transpose(outgoing, (2, 3, 1, 0, 4))
    arrived = lax.all_to_all(
        outgoing.reshape(blocks * cd_size, occ_dev * group_size * group_size),
        ("ab", "cd"),
        split_axis=0,
        concat_axis=0,
        tiled=True,
    )
    arrived = arrived.reshape(blocks, cd_size, occ_dev, group_size, group_size)
    mirrored = jnp.transpose(arrived, (2, 4, 0, 1, 3)).reshape(
        occ_dev, group_size, blocks * block_size
    )
    partner = from_partner(mirrored, "ij", 0)
    return (direct + partner).reshape(occ_dev, 1, group_size, blocks * block_size)


def per_device(amplitudes, integrals, tile_row, tile_col, tile_count):
    n_ab = lax.axis_size("ab")
    if (
        amplitudes.shape[1] == integrals.shape[1]
        and integrals.shape[0] == n_ab * n_ab
        and lax.axis_size("ij") == 2
        and amplitudes.shape[0] % LANES == 0
    ):
        return fused(amplitudes, integrals, tile_row, tile_col, tile_count)
    return general(amplitudes, integrals, tile_row, tile_col, tile_count)


def solution(mesh):
    in_specs = (
        P("ij", ("cd", "ab")),
        P(("ab", "cd"), None, None),
        P(("ab", "cd")),
        P(("ab", "cd")),
        P(("ab", "cd")),
    )
    out_specs = P("ij", "ab", "cd", None)
    return jax.shard_map(
        per_device, mesh=mesh, in_specs=in_specs, out_specs=out_specs, check_vma=False
    )
```

profile of v0, /device:TPU:1, one launch (start us, length us, event | category | flops | bytes accessed | tf_op | source)
XLA Modules:
  0.0 47.5 jit_solution(1092443357457127831)
XLA Ops:
  0.7 45.2 %shard_map.55 = f32[4,64,256]{2,1,0:T(8,128)} custom-call(s32[16]{0:T(128)} %row_ref.1, s32[16]{0:T(128)} %col_ref.1, s32[1]{0:T(128)S(6)} %copy.7.count_ref, f32[256,256]{1,0:T(8,128)} %amp_ref.1, f32[16,256,256]{2,1,0:T(8,128)} %tiles_ref.1), custom_call_target="tpu_custom_call" | custom-call | tf_op jit(solution)/shard_map/pallas_call | solution.py:256
  45.8 1.7 %copy.8 = f32[256,1,4,64]{0,3,2,1:T(8,128)} copy(f32[256,1,4,64]{0,3,2,1:T(8,128)} %bitcast.3) | data formatting | bytes 524288
where the time goes:
time: 47.7 us; the launch traced here: 47.5 us
  Pallas kernels  45.2 us (95%)
  local copies, waits for them, and re-layouts  1.67 us (4%)
  between operations  0.66 us (1%)
    pallas_call x1, Pallas kernels, fused(): pl.pallas_call(functools.partial(ladder_kernel, n_ab, n_cd, block, chunks...  45.2 us
    unnamed x1, local copies, waits for them, and re-layouts  1.67 us

commit v1 on v0

v1 whole, which is shorter than its diff:
```python
import functools
import math

import jax
import jax.numpy as jnp
from jax import lax
from jax.experimental import pallas as pl
from jax.experimental.pallas import tpu as pltpu
from jax.sharding import PartitionSpec as P

MESH = pl.DeviceIdType.MESH
LANES = 128
VMEM_BYTES = 63 * 1024 * 1024


def split(value):
    high = value.astype(jnp.bfloat16)
    low = (value - high.astype(jnp.float32)).astype(jnp.bfloat16)
    return high, low


def ladder_kernel(
    n_ab, n_cd, block,
    row_ref, col_ref, count_ref, amp_ref, tiles_ref, out_ref,
    tiles, w_high, w_low, gathered, a_both, partial, mirror_out, mirror_in, z_in, relayed,
    summed, outgoing, mirrored, result, traded,
    tile_sem, own_sem, ag_send, ag_recv, x_send, x_recv, z_send, z_recv,
    mi_send, mi_recv, tr_send, tr_recv,
):
    me_ab, me_cd, me_ij = lax.axis_index("ab"), lax.axis_index("cd"), lax.axis_index("ij")
    slots, size = tiles_ref.shape[0], tiles_ref.shape[1]
    steps = partial.shape[0]
    half = LANES // 2
    group = block // n_cd
    width = n_ab * block
    rows = group * width
    targets = n_ab * n_cd
    piece = group * group
    own_place = me_ab * n_cd + me_cd
    near = [me_ab, me_ab + 1 - 2 * lax.rem(me_ab, 2), lax.rem(me_ab + 2, n_ab), n_ab - 1 - me_ab]
    low_side = me_cd < n_cd // 2
    outer = (me_cd == 0) | (me_cd == n_cd - 1)
    inner = (me_cd > 0) & (me_cd < n_cd - 1)
    far = jnp.where(low_side, n_cd - 1, 0)
    next_in = jnp.where(low_side, 1, 2)
    order = [
        far,
        jnp.where(outer, n_cd - 1 - next_in, n_cd - 1 - far),
        jnp.where(outer, next_in, n_cd - 1 - me_cd),
        me_cd,
    ]
    z_device = [
        far,
        jnp.where(outer, next_in, n_cd - 1 - far),
        jnp.where(outer, next_in, n_cd - 1 - me_cd),
    ]
    z_slot = [jnp.where(outer, 0, 2), jnp.where(outer, 3, 1), jnp.where(outer, 0, 1)]

    tile_copies = [
        pltpu.make_async_copy(tiles_ref.at[k], tiles.at[k], tile_sem.at[k]) for k in range(slots)
    ]
    for copy in tile_copies:
        copy.start()

    barrier = pltpu.get_barrier_semaphore()
    for j in range(1, n_ab):
        for core in range(2):
            pl.semaphore_signal(
                barrier, inc=1, device_id=(near[j], me_cd, core), device_id_type=MESH
            )
    pl.semaphore_signal(barrier, inc=1, device_id=(me_ab, me_cd, 1 - me_ij), device_id_type=MESH)
    for m in range(1, n_cd):
        pl.semaphore_signal(
            barrier, inc=1, device_id=(me_ab, lax.rem(me_cd + m, n_cd), me_ij), device_id_type=MESH
        )
    pl.semaphore_wait(barrier, 2 * (n_ab - 1) + 1 + n_cd - 1)

    def spread(s, core, j):
        return pltpu.make_async_remote_copy(
            src_ref=amp_ref.at[pl.ds((2 * s + core) * half, half)],
            dst_ref=gathered.at[s, j, pl.ds(me_ij * half, half)],
            send_sem=ag_send.at[s, core, j],
            recv_sem=ag_recv.at[s, j, me_ij],
            device_id=(near[j], me_cd, core),
            device_id_type=MESH,
        )

    def arrival(s, j, h):
        return pltpu.make_async_remote_copy(
            src_ref=amp_ref.at[pl.ds(0, half)],
            dst_ref=gathered.at[s, j, pl.ds(h * half, half)],
            send_sem=ag_send.at[s, 0, j],
            recv_sem=ag_recv.at[s, j, h],
            device_id=(near[j], me_cd, me_ij),
            device_id_type=MESH,
        )

    def keep(s, core):
        return pltpu.make_async_copy(
            amp_ref.at[pl.ds((2 * s + core) * half, half)],
            gathered.at[s, 0, pl.ds(core * half, half)],
            own_sem.at[s],
        )

    for s in range(steps):
        for core in range(2):
            for j in (3, 1, 2):
                spread(s, core, j).start()

            @pl.when(me_ij == core)
            def _():
                keep(s, core).start()

            @pl.when(me_ij != core)
            def _():
                spread(s, core, 0).start()

    keys = [row_ref[k] * n_ab + col_ref[k] for k in range(slots)]
    live_count = count_ref[0]
    for copy in tile_copies:
        copy.wait()
    for j in range(n_ab):
        column = near[j]
        for r in range(n_ab):
            slot = jnp.int32(0)
            for k in range(1, slots):
                slot = jnp.where(keys[k] == r * n_ab + column, jnp.int32(k), slot)
            scale = jnp.where(slot < live_count, jnp.float32(1), jnp.float32(0))
            high, low = split(tiles[slot] * scale)
            at = (slice(None), pl.ds(r * block, block), pl.ds(j * size, size))
            w_high[at] = high.reshape(block, block, size)
            w_low[at] = low.reshape(block, block, size)

    contract = (((1,), (1,)), ((), ()))

    def to_plane(s, i):
        source = partial.at[s, pl.ds(order[i] * rows, rows)]
        return pltpu.make_async_remote_copy(
            src_ref=source,
            dst_ref=z_in.at[s, z_slot[i]],
            send_sem=z_send.at[s, i],
            recv_sem=z_recv.at[s, z_slot[i]],
            device_id=(me_ab, z_device[i], me_ij),
            device_id_type=MESH,
        )

    def passed_on(s):
        return pltpu.make_async_remote_copy(
            src_ref=relayed.at[s],
            dst_ref=z_in.at[s, 1],
            send_sem=z_send.at[s, 2],
            recv_sem=z_recv.at[s, 1],
            device_id=(me_ab, z_device[2], me_ij),
            device_id_type=MESH,
        )

    def from_plane(s, place):
        return pltpu.make_async_remote_copy(
            src_ref=relayed.at[s],
            dst_ref=z_in.at[s, place],
            send_sem=z_send.at[s, 0],
            recv_sem=z_recv.at[s, place],
            device_id=(me_ab, z_device[0], me_ij),
            device_id_type=MESH,
        )

    def send_plane(s, i):
        if i < 2:
            to_plane(s, i).start()
        elif i == 2:

            @pl.when(outer)
            def _():
                to_plane(s, i).start()

    def gather(s):
        for j in range(n_ab):
            if j:
                arrival(s, j, 0).wait_recv()
                arrival(s, j, 1).wait_recv()
            else:

                @pl.when(me_ij == 0)
                def _():
                    keep(s, 0).wait()
                    arrival(s, 0, 1).wait_recv()

                @pl.when(me_ij == 1)
                def _():
                    keep(s, 1).wait()
                    arrival(s, 0, 0).wait_recv()

            high, low = split(gathered[s, j])
            a_both[pl.ds(0, LANES), pl.ds(j * size, size)] = high
            a_both[pl.ds(LANES, LANES), pl.ds(j * size, size)] = low

    def compute(s, send):
        for i in range(n_cd):
            d = order[i]
            lead = pl.ds(d * group, group)
            left_high = w_high[lead].reshape(rows, n_ab * size)
            left_low = w_low[lead].reshape(rows, n_ab * size)
            right = a_both[...]
            wide = lax.dot_general(left_high, right, contract, preferred_element_type=jnp.float32)
            value = wide[:, LANES:] + lax.dot_general(
                left_low, right[:LANES], contract, preferred_element_type=jnp.float32
            )
            value += wide[:, :LANES]
            partial[s, pl.ds(d * rows, rows)] = value
            if send:
                send_plane(s, i)
            else:
                for j in range(n_ab):
                    for x in range(group):
                        mirror_out[j, pl.ds(d * group + x, block, stride=block), :] = pltpu.roll(
                            partial[s, pl.ds(d * rows + x * width + near[j] * block, block)], half, 1
                        )

    def across(j, i):
        part = pl.ds(order[i] * group * block, group * block)
        return pltpu.make_async_remote_copy(
            src_ref=mirror_out.at[j, part],
            dst_ref=mirror_in.at[j, part],
            send_sem=x_send.at[j, i],
            recv_sem=x_recv.at[j, i],
            device_id=(near[j], me_cd, me_ij),
            device_id_type=MESH,
        )

    def add_mirrors(s):
        for i in range(n_cd):
            d = order[i]
            for j in range(n_ab):
                source = mirror_out if j == 0 else mirror_in
                if j:
                    across(j, i).wait_recv()
                for x in range(group):
                    at = pl.ds(d * rows + x * width + near[j] * block, block)
                    partial[s, at] += source[j, pl.ds((d * group + x) * block, block)]
            send_plane(s, i)

    def relay(s):
        @pl.when(inner)
        def _():
            from_plane(s, 3).wait_recv()
            relayed[s] = partial[s, pl.ds(order[2] * rows, rows)] + z_in[s, 3]
            passed_on(s).start()

    def total(s, into):
        from_plane(s, 0).wait_recv()
        from_plane(s, 1).wait_recv()
        into[s] = partial[s, pl.ds(me_cd * rows, rows)] + z_in[s, 0] + z_in[s, 1]

        @pl.when(outer)
        def _():
            from_plane(s, 2).wait_recv()
            into[s] += z_in[s, 2]

    def mirror_copy(s, j, m):
        q = lax.rem(me_cd + m, n_cd)
        return pltpu.make_async_remote_copy(
            src_ref=outgoing.at[s, pl.ds((near[j] * n_cd + q) * piece, piece)],
            dst_ref=mirrored.at[s, pl.ds(own_place * piece, piece)],
            send_sem=mi_send.at[s, j, m],
            recv_sem=mi_recv.at[s, j, m],
            device_id=(near[j], q, me_ij),
            device_id_type=MESH,
        )

    def mirror_arrival(s, j, m):
        place = near[j] * n_cd + lax.rem(me_cd - m + n_cd, n_cd)
        return pltpu.make_async_remote_copy(
            src_ref=outgoing.at[s, pl.ds(0, piece)],
            dst_ref=mirrored.at[s, pl.ds(place * piece, piece)],
            send_sem=mi_send.at[s, j, m],
            recv_sem=mi_recv.at[s, j, m],
            device_id=(near[j], lax.rem(me_cd + m, n_cd), me_ij),
            device_id_type=MESH,
        )

    others = [(j, m) for j in (3, 1, 2, 0) for m in (2, 3, 1, 0) if j or m]

    def send_mirrors(s):
        for x in range(group):
            for y in range(group):
                outgoing[s, pl.ds(x * group + y, targets, stride=piece), :] = pltpu.roll(
                    summed[s, pl.ds(x * width + y, targets, stride=group), :], half, 1
                )
        for j, m in others:
            mirror_copy(s, j, m).start()
        here = pl.ds(own_place * piece, piece)
        mirrored[s, here] = outgoing[s, here]

    def take_mirrors(s):
        for j, m in others:
            mirror_arrival(s, j, m).wait_recv()
        for y in range(group):
            at = pl.ds(y * width, width)
            result[s, at] = summed[s, at] + mirrored[s, pl.ds(y, width, stride=group), :]

    def trade(s):
        return pltpu.make_async_remote_copy(
            src_ref=result.at[s],
            dst_ref=traded.at[s],
            send_sem=tr_send.at[s],
            recv_sem=tr_recv.at[s],
            device_id=(me_ab, me_cd, 1 - me_ij),
            device_id_type=MESH,
        )

    def store(s):
        trade(s).wait_recv()
        lane = lax.broadcasted_iota(jnp.int32, (width, LANES), 1)
        mine = (lane >= half) == (me_ij == 1)
        for y in range(group):
            at = pl.ds(y * width, width)
            out_ref[y, :, pl.ds(s * LANES, LANES)] = jnp.where(
                mine, result[s, at], pltpu.roll(traded[s, at], half, 1)
            )

    last = steps - 1
    for s in range(last):
        gather(s)
        compute(s, True)
        relay(s)
    gather(last)
    compute(last, False)
    for i in range(n_cd):
        for j in (3, 1, 2):
            across(j, i).start()
    for s in range(last):
        total(s, summed)
        send_mirrors(s)
    add_mirrors(last)
    relay(last)
    for s in range(last):
        take_mirrors(s)
        trade(s).start()
    total(last, result)
    trade(last).start()
    for s in range(steps):
        store(s)

    for s in range(steps):
        trade(s).wait_send()
        for core in range(2):
            for j in range(1, n_ab):
                spread(s, core, j).wait_send()

            @pl.when(me_ij != core)
            def _():
                spread(s, core, 0).wait_send()

        for i in range(3):
            to_plane(s, i).wait_send()
    for i in range(n_cd):
        for j in range(1, n_ab):
            across(j, i).wait_send()
    for s in range(last):
        for j, m in others:
            mirror_copy(s, j, m).wait_send()


def fused(amplitudes, integrals, tile_row, tile_col, tile_count):
    occ_dev = amplitudes.shape[0]
    slots, size = integrals.shape[0], integrals.shape[1]
    block = math.isqrt(size)
    n_ab, n_cd = lax.axis_size("ab"), lax.axis_size("cd")
    group = block // n_cd
    rows = group * n_ab * block
    steps = occ_dev // LANES
    targets = n_ab * n_cd
    piece = group * group
    f32, bf16 = jnp.float32, jnp.bfloat16
    dma = pltpu.SemaphoreType.DMA
    out = pl.pallas_call(
        functools.partial(ladder_kernel, n_ab, n_cd, block),
        out_shape=jax.ShapeDtypeStruct((group, n_ab * block, occ_dev), f32),
        in_specs=[pl.BlockSpec(memory_space=pltpu.SMEM)] * 3
        + [pl.BlockSpec(memory_space=pl.ANY)] * 2,
        out_specs=pl.BlockSpec(memory_space=pltpu.VMEM),
        scratch_shapes=[
            pltpu.VMEM((slots, size, size), f32),
            pltpu.VMEM((block, n_ab * block, n_ab * size), bf16),
            pltpu.VMEM((block, n_ab * block, n_ab * size), bf16),
            pltpu.VMEM((steps, n_ab, LANES, size), f32),
            pltpu.VMEM((2 * LANES, n_ab * size), bf16),
            pltpu.VMEM((steps, n_cd * rows, LANES), f32),
            pltpu.VMEM((n_ab, size, LANES), f32),
            pltpu.VMEM((n_ab, size, LANES), f32),
            pltpu.VMEM((steps, 4, rows, LANES), f32),
            pltpu.VMEM((steps, rows, LANES), f32),
            pltpu.VMEM((steps, rows, LANES), f32),
            pltpu.VMEM((steps, targets * piece, LANES), f32),
            pltpu.VMEM((steps, targets * piece, LANES), f32),
            pltpu.VMEM((steps, rows, LANES), f32),
            pltpu.VMEM((steps, rows, LANES), f32),
            dma((slots,)),
            dma((steps,)),
            dma((steps, 2, n_ab)),
            dma((steps, n_ab, 2)),
            dma((n_ab, n_cd)),
            dma((n_ab, n_cd)),
            dma((steps, 3)),
            dma((steps, 4)),
            dma((steps, n_ab, n_cd)),
            dma((steps, n_ab, n_cd)),
            dma((steps,)),
            dma((steps,)),
        ],
        compiler_params=pltpu.CompilerParams(
            collective_id=0, has_side_effects=True, vmem_limit_bytes=VMEM_BYTES
        ),
    )(tile_row, tile_col, tile_count, amplitudes, integrals)
    return jnp.transpose(out, (2, 0, 1))[:, None]


def from_partner(block, axis, bit):
    count = lax.axis_size(axis)
    route = []
    for low in range(count):
        high = low | 1 << bit
        if high != low and high < count:
            route += [(low, high), (high, low)]
    return lax.ppermute(block, axis, route)


def place_rows(chosen, tile_rows, row_picks, block_size):
    terms = jnp.einsum("okf,kef->oke", chosen, tile_rows, precision=lax.Precision.HIGHEST)
    occ_dev, slots, width = terms.shape
    terms = terms.reshape(occ_dev, slots, width // block_size, block_size)
    placed = jnp.einsum("rk,okab->aorb", row_picks, terms, precision=lax.Precision.HIGHEST)
    return placed.reshape(width // block_size, occ_dev, row_picks.shape[0] * block_size)


def general(amplitudes, integrals, tile_row, tile_col, tile_count):
    occ_dev = amplitudes.shape[0]
    slots = integrals.shape[0]
    tile_size = integrals.shape[1]
    block_size = math.isqrt(tile_size)
    blocks = lax.axis_size("ab")
    cd_size = lax.axis_size("cd")
    group_size = block_size // cd_size
    live_count = tile_count[0]
    live = jnp.arange(slots, dtype=jnp.int32) < live_count
    row_picks = (
        (tile_row[None, :] == jnp.arange(blocks, dtype=jnp.int32)[:, None]) & live[None, :]
    ).astype(jnp.float32)
    gathered = lax.all_gather(amplitudes, "ab", axis=1, tiled=True)
    columns = gathered.reshape(occ_dev, -1, tile_size)
    chosen = jnp.take(columns, tile_col, axis=1)
    partial_value = place_rows(chosen, integrals, row_picks, block_size)
    summed = lax.psum_scatter(partial_value, "cd", scatter_dimension=0, tiled=True)
    direct = jnp.transpose(summed, (1, 0, 2))
    outgoing = summed.reshape(group_size, occ_dev, blocks, cd_size, group_size)
    outgoing = jnp.transpose(outgoing, (2, 3, 1, 0, 4))
    arrived = lax.all_to_all(
        outgoing.reshape(blocks * cd_size, occ_dev * group_size * group_size),
        ("ab", "cd"),
        split_axis=0,
        concat_axis=0,
        tiled=True,
    )
    arrived = arrived.reshape(blocks, cd_size, occ_dev, group_size, group_size)
    mirrored = jnp.transpose(arrived, (2, 4, 0, 1, 3)).reshape(
        occ_dev, group_size, blocks * block_size
    )
    partner = from_partner(mirrored, "ij", 0)
    return (direct + partner).reshape(occ_dev, 1, group_size, blocks * block_size)


def per_device(amplitudes, integrals, tile_row, tile_col, tile_count):
    n_ab = lax.axis_size("ab")
    if (
        amplitudes.shape[1] == integrals.shape[1]
        and integrals.shape[0] == n_ab * n_ab
        and n_ab == 4
        and lax.axis_size("cd") == 4
        and lax.axis_size("ij") == 2
        and amplitudes.shape[0] % LANES == 0
    ):
        return fused(amplitudes, integrals, tile_row, tile_col, tile_count)
    return general(amplitudes, integrals, tile_row, tile_col, tile_count)


def solution(mesh):
    in_specs = (
        P("ij", ("cd", "ab")),
        P(("ab", "cd"), None, None),
        P(("ab", "cd")),
        P(("ab", "cd")),
        P(("ab", "cd")),
    )
    out_specs = P("ij", "ab", "cd", None)
    return jax.shard_map(
        per_device, mesh=mesh, in_specs=in_specs, out_specs=out_specs, check_vma=False
    )
```

time: 47.7 us -> 42.6 us (0.89); the launches traced: 47.5 us -> 41.8 us
  Pallas kernels: 45.2 us -> 39.5 us
    pallas_call x1, Pallas kernels: 45.2 us -> 39.5 us  [fused(): pl.pallas_call(functools.partial(ladder_kernel, n_ab, n_cd, block), out_s...]
where the time goes in v1:
time: 42.6 us; the launch traced here: 41.8 us
  Pallas kernels  39.5 us (93%)
  local copies, waits for them, and re-layouts  1.67 us (4%)
  between operations  0.66 us (2%)
    pallas_call x1, Pallas kernels, fused(): pl.pallas_call(functools.partial(ladder_kernel, n_ab, n_cd, block), out_s...  39.5 us
    unnamed x1, local copies, waits for them, and re-layouts  1.67 us

profile of v1, /device:TPU:1, one launch (start us, length us, event | category | flops | bytes accessed | tf_op | source)
XLA Modules:
  0.0 41.8 jit_solution(17605703875294423821)
XLA Ops:
  0.7 39.5 %shard_map.55 = f32[4,64,256]{2,1,0:T(8,128)} custom-call(s32[16]{0:T(128)} %row_ref.1, s32[16]{0:T(128)} %col_ref.1, s32[1]{0:T(128)S(6)} %copy.7.count_ref, f32[256,256]{1,0:T(8,128)} %amp_ref.1, f32[16,256,256]{2,1,0:T(8,128)} %tiles_ref.1), custom_call_target="tpu_custom_call" | custom-call | tf_op jit(solution)/shard_map/pallas_call | solution.py:376
  40.2 1.7 %copy.8 = f32[256,1,4,64]{0,3,2,1:T(8,128)} copy(f32[256,1,4,64]{0,3,2,1:T(8,128)} %bitcast.3) | data formatting | bytes 524288

commit v2 on v1

--- a/solution.py
+++ b/solution.py
@@ -44,17 +44,17 @@
     far = jnp.where(low_side, n_cd - 1, 0)
     next_in = jnp.where(low_side, 1, 2)
     order = [
-        far,
-        jnp.where(outer, n_cd - 1 - next_in, n_cd - 1 - far),
+        jnp.where(outer, n_cd - 1 - next_in, far),
+        jnp.where(outer, far, n_cd - 1 - far),
         jnp.where(outer, next_in, n_cd - 1 - me_cd),
         me_cd,
     ]
     z_device = [
-        far,
-        jnp.where(outer, next_in, n_cd - 1 - far),
+        jnp.where(outer, next_in, far),
+        jnp.where(outer, far, n_cd - 1 - far),
         jnp.where(outer, next_in, n_cd - 1 - me_cd),
     ]
-    z_slot = [jnp.where(outer, 0, 2), jnp.where(outer, 3, 1), jnp.where(outer, 0, 1)]
+    z_slot = [jnp.where(outer, 3, 2), jnp.where(outer, 0, 1), jnp.where(outer, 0, 1)]
 
     tile_copies = [
         pltpu.make_async_copy(tiles_ref.at[k], tiles.at[k], tile_sem.at[k]) for k in range(slots)
@@ -336,11 +336,11 @@
     for s in range(last):
         take_mirrors(s)
         trade(s).start()
+    for s in range(last):
+        store(s)
     total(last, result)
     trade(last).start()
-    for s in range(steps):
-        store(s)
-
+    store(last)
     for s in range(steps):
         trade(s).wait_send()
         for core in range(2):

time: 42.6 us -> 41.1 us (0.965)
  Pallas kernels: 39.5 us -> 38.2 us
    pallas_call x1, Pallas kernels: 39.5 us -> 38.2 us  [fused(): pl.pallas_call(functools.partial(ladder_kernel, n_ab, n_cd, block), out_s...]
where the time goes in v2:
time: 41.1 us; the launch traced here: 40.6 us
  Pallas kernels  38.2 us (93%)
  local copies, waits for them, and re-layouts  1.67 us (4%)
  between operations  0.66 us (2%)
    pallas_call x1, Pallas kernels, fused(): pl.pallas_call(functools.partial(ladder_kernel, n_ab, n_cd, block), out_s...  38.2 us
    unnamed x1, local copies, waits for them, and re-layouts  1.67 us

profile of v2, /device:TPU:1, one launch (start us, length us, event | category | flops | bytes accessed | tf_op | source)
XLA Modules:
  0.0 40.6 jit_solution(14428150767512884235)
XLA Ops:
  0.7 38.2 %shard_map.55 = f32[4,64,256]{2,1,0:T(8,128)} custom-call(s32[16]{0:T(128)} %row_ref.1, s32[16]{0:T(128)} %col_ref.1, s32[1]{0:T(128)S(6)} %copy.7.count_ref, f32[256,256]{1,0:T(8,128)} %amp_ref.1, f32[16,256,256]{2,1,0:T(8,128)} %tiles_ref.1), custom_call_target="tpu_custom_call" | custom-call | tf_op jit(solution)/shard_map/pallas_call | solution.py:376
  38.9 1.7 %copy.8 = f32[256,1,4,64]{0,3,2,1:T(8,128)} copy(f32[256,1,4,64]{0,3,2,1:T(8,128)} %bitcast.3) | data formatting | bytes 524288

commit v3 on v2

--- a/solution.py
+++ b/solution.py
@@ -10,7 +10,7 @@
 
 MESH = pl.DeviceIdType.MESH
 LANES = 128
-VMEM_BYTES = 63 * 1024 * 1024
+VMEM_BYTES = 54848 * 1024
 
 
 def split(value):
@@ -21,7 +21,7 @@
 
 def ladder_kernel(
     n_ab, n_cd, block,
-    row_ref, col_ref, count_ref, amp_ref, tiles_ref, out_ref,
+    key_ref, amp_ref, tiles_ref, out_ref,
     tiles, w_high, w_low, gathered, a_both, partial, mirror_out, mirror_in, z_in, relayed,
     summed, outgoing, mirrored, result, traded,
     tile_sem, own_sem, ag_send, ag_recv, x_send, x_recv, z_send, z_recv,
@@ -115,18 +115,17 @@
             def _():
                 spread(s, core, 0).start()
 
-    keys = [row_ref[k] * n_ab + col_ref[k] for k in range(slots)]
-    live_count = count_ref[0]
+    keys = [key_ref[k] for k in range(slots)]
     for copy in tile_copies:
         copy.wait()
     for j in range(n_ab):
         column = near[j]
         for r in range(n_ab):
-            slot = jnp.int32(0)
-            for k in range(1, slots):
+            slot = jnp.int32(slots)
+            for k in range(slots):
                 slot = jnp.where(keys[k] == r * n_ab + column, jnp.int32(k), slot)
-            scale = jnp.where(slot < live_count, jnp.float32(1), jnp.float32(0))
-            high, low = split(tiles[slot] * scale)
+            scale = jnp.where(slot < slots, jnp.float32(1), jnp.float32(0))
+            high, low = split(tiles[jnp.minimum(slot, slots - 1)] * scale)
             at = (slice(None), pl.ds(r * block, block), pl.ds(j * size, size))
             w_high[at] = high.reshape(block, block, size)
             w_low[at] = low.reshape(block, block, size)
@@ -373,10 +372,12 @@
     piece = group * group
     f32, bf16 = jnp.float32, jnp.bfloat16
     dma = pltpu.SemaphoreType.DMA
+    live = jnp.arange(slots, dtype=jnp.int32) < tile_count[0]
+    keys = jnp.where(live, tile_row * n_ab + tile_col, jnp.int32(-1))
     out = pl.pallas_call(
         functools.partial(ladder_kernel, n_ab, n_cd, block),
         out_shape=jax.ShapeDtypeStruct((group, n_ab * block, occ_dev), f32),
-        in_specs=[pl.BlockSpec(memory_space=pltpu.SMEM)] * 3
+        in_specs=[pl.BlockSpec(memory_space=pltpu.SMEM)]
         + [pl.BlockSpec(memory_space=pl.ANY)] * 2,
         out_specs=pl.BlockSpec(memory_space=pltpu.VMEM),
         scratch_shapes=[
@@ -411,7 +412,7 @@
         compiler_params=pltpu.CompilerParams(
             collective_id=0, has_side_effects=True, vmem_limit_bytes=VMEM_BYTES
         ),
-    )(tile_row, tile_col, tile_count, amplitudes, integrals)
+    )(keys, amplitudes, integrals)
     return jnp.transpose(out, (2, 0, 1))[:, None]
 
 

time: 41.1 us -> 39.9 us (0.971)
  local copies, waits for them, and re-layouts: 1.67 us -> 0.71 us
  Pallas kernels: 38.2 us -> 37.4 us
  other arithmetic: 0 us -> 0.68 us
    unnamed x1, local copies, waits for them, and re-layouts: 1.67 us -> 0.71 us
    pallas_call x1, Pallas kernels: 38.2 us -> 37.4 us  [fused(): pl.pallas_call(functools.partial(ladder_kernel, n_ab, n_cd, block), out_s...]
    select_n x0 -> x1, other arithmetic: none -> 0.68 us  [fused(): keys = jnp.where(live, tile_row * n_ab + tile_col, jnp.int32(-1))]
where the time goes in v3:
time: 39.9 us; the launch traced here: 39.4 us
  Pallas kernels  37.4 us (94%)
  local copies, waits for them, and re-layouts  0.71 us (2%)
  other arithmetic  0.68 us (2%)
  between operations  0.66 us (2%)
    pallas_call x1, Pallas kernels, fused(): pl.pallas_call(functools.partial(ladder_kernel, n_ab, n_cd, block), out_s...  37.4 us

profile of v3, /device:TPU:1, one launch (start us, length us, event | category | flops | bytes accessed | tf_op | source)
XLA Modules:
  0.0 39.4 jit_solution(8088523192620978480)
XLA Ops:
  0.7 0.7 %compare_select_fusion.key_ref = s32[16]{0:T(128)S(1)} fusion(s32[16]{0:T(128)} %param.8, s32[16]{0:T(128)} %param.7, s32[]{:T(128)} %bitcast.4), kind=kLoop, calls=%fused_computation | loop fusion | flops 64 | bytes 196 | tf_op jit(solution)/shard_map/jit(_where)/select_n | solution.py:376
  1.3 37.4 %shard_map.55 = f32[4,64,256]{2,1,0:T(8,128)S(1)} custom-call(s32[16]{0:T(128)S(1)} %compare_select_fusion.key_ref, f32[256,256]{1,0:T(8,128)} %amp_ref.1, f32[16,256,256]{2,1,0:T(8,128)} %tiles_ref.1), custom_call_target="tpu_custom_call" | custom-call | tf_op jit(solution)/shard_map/pallas_call | solution.py:377
  38.7 0.7 %copy.8 = f32[256,1,4,64]{0,3,2,1:T(8,128)} copy(f32[256,1,4,64]{0,3,2,1:T(8,128)S(1)} %bitcast.5) | data formatting | bytes 524288
